TPU v7x, 1024 devices: a whole 4x8x16 slice. The times are simulated.
1024 devices in a mesh: seq: 64 (over z, y_lo, core), chan: 16 (over y_hi, x).
Axes of the slice: x: 4, y: 8 (y_hi: 4, y_lo: 2; y = y_hi * 2 + y_lo), z: 16, core: 2. Of those that a mesh axis runs over, the one named last changes fastest.
Arguments:
- values: bfloat16 [16384, 4096], P('seq', 'chan'), may hold values from -6 to 6
- gate_in: bfloat16 [16384, 4096], P('seq', 'chan'), may hold values from -6 to 6
- gate_out: bfloat16 [16384, 4096], P('seq', 'chan'), may hold values from -6 to 6
- spectrum: float32 [2, 16, 1024, 4096], P(None, None, 'seq', 'chan'), may hold values from -6 to 6
- out_weight: bfloat16 [4096, 8192], P('chan'), may hold values from -0.125 to 0.125
Outputs:
- mixed: bfloat16 [16384, 8192], P('seq', 'chan')
All inputs are finite; a program needn't handle non-finite values.
Results may differ from a plain program's by a relative error of at most 0.024.
Values may be sent and summed in bfloat16 or wider, within the bound.
A program may use at most 64 MiB of HBM per device.

v0:
```python
import math

import jax
import jax.numpy as jnp
from jax import lax
from jax.sharding import PartitionSpec as P

BLOCK = 1024


def angle_table(first, second, period):
    product = first[:, None] * second[None, :] % period
    return product.astype(jnp.float32) * (2.0 * math.pi / period)


def to_columns(data):
    return lax.all_to_all(data, "seq", split_axis=2, concat_axis=1, tiled=True)


def to_rows(data):
    return lax.all_to_all(data, "seq", split_axis=1, concat_axis=2, tiled=True)


def shards(values, gate_in, gate_out, spectrum, out_weight):
    seq_count = lax.axis_size("seq")
    seq_index = lax.axis_index("seq")
    tok_rows, chan_width = values.shape
    block_len = BLOCK
    block_rows = block_len // seq_count
    span = tok_rows // block_rows
    tokens_all = block_len * span
    col_share = span * chan_width // seq_count
    full_block = jnp.arange(block_len, dtype=jnp.int32)
    full_span = jnp.arange(span, dtype=jnp.int32)
    block_angle = angle_table(full_block, full_block, block_len)
    block_cos = jnp.cos(block_angle).astype(jnp.bfloat16)
    block_sin = jnp.sin(block_angle).astype(jnp.bfloat16)
    span_angle = angle_table(full_span, full_span, span)
    span_cos = jnp.cos(span_angle).astype(jnp.bfloat16)
    span_sin = jnp.sin(span_angle).astype(jnp.bfloat16)
    source = (values.astype(jnp.float32) * gate_in.astype(jnp.float32)).astype(jnp.bfloat16)
    spread = to_columns(source.reshape(1, block_rows, seq_count, col_share))
    columns = spread.reshape(block_len, col_share)
    cos_part = jnp.dot(jnp.transpose(block_cos), columns, preferred_element_type=jnp.float32)
    sin_part = jnp.dot(jnp.transpose(block_sin), columns, preferred_element_type=jnp.float32)
    col_pos = (seq_index * col_share + jnp.arange(col_share, dtype=jnp.int32)) // chan_width
    turn = angle_table(full_block, col_pos, tokens_all)
    turn_cos = jnp.cos(turn)
    turn_sin = jnp.sin(turn)
    twist_re = cos_part * turn_cos - sin_part * turn_sin
    twist_im = -sin_part * turn_cos - cos_part * turn_sin
    twisted = jnp.stack([twist_re, twist_im]).astype(jnp.bfloat16)
    arranged = to_rows(twisted).reshape(2, block_rows, span, chan_width)
    with_cos = jnp.einsum("bd,kcbh->kdch", span_cos, arranged, preferred_element_type=jnp.float32)
    with_sin = jnp.einsum("bd,kcbh->kdch", span_sin, arranged, preferred_element_type=jnp.float32)
    freq_re = with_cos[0] + with_sin[1]
    freq_im = with_cos[1] - with_sin[0]
    prod_re = freq_re * spectrum[0] - freq_im * spectrum[1]
    prod_im = freq_re * spectrum[1] + freq_im * spectrum[0]
    product = jnp.stack([prod_re, prod_im]).astype(jnp.bfloat16)
    back_cos = jnp.einsum("db,kdch->kcbh", span_cos, product, preferred_element_type=jnp.float32)
    back_sin = jnp.einsum("db,kdch->kcbh", span_sin, product, preferred_element_type=jnp.float32)
    back_re = (back_cos[0] - back_sin[1]) / span
    back_im = (back_cos[1] + back_sin[0]) / span
    local_freq = seq_index * block_rows + jnp.arange(block_rows, dtype=jnp.int32)
    turn_back = angle_table(local_freq, full_span, tokens_all)
    back_tc = jnp.cos(turn_back)[:, :, None]
    back_ts = jnp.sin(turn_back)[:, :, None]
    rotated = jnp.stack(
        [back_re * back_tc - back_im * back_ts, back_im * back_tc + back_re * back_ts]
    ).astype(jnp.bfloat16)
    gathered = to_columns(rotated.reshape(2, block_rows, seq_count, col_share)).reshape(
        2, block_len, col_share
    )
    summed = jnp.dot(block_cos, gathered[0], preferred_element_type=jnp.float32)
    summed = summed - jnp.dot(block_sin, gathered[1], preferred_element_type=jnp.float32)
    ordered = (summed / block_len).astype(jnp.bfloat16).reshape(1, block_len, col_share)
    conv = to_rows(ordered).reshape(tok_rows, chan_width)
    gated = (conv.astype(jnp.float32) * gate_out.astype(jnp.float32)).astype(jnp.bfloat16)
    partial_sum = jnp.dot(gated, out_weight, preferred_element_type=jnp.float32)
    mixed = lax.psum_scatter(
        partial_sum.astype(jnp.bfloat16), "chan", scatter_dimension=1, tiled=True
    )
    return mixed


def solution(mesh):
    placed = (
        P("seq", "chan"),
        P("seq", "chan"),
        P("seq", "chan"),
        P(None, None, "seq", "chan"),
        P("chan", None),
    )
    return jax.shard_map(
        shards, mesh=mesh, in_specs=placed, out_specs=P("seq", "chan"), check_vma=False
    )
```

profile of v0, /device:TPU:1, one launch (start us, length us, event | category | flops | bytes accessed | tf_op | source)
XLA Modules:
  0.0 311.6 jit_solution(15480910430944726635)
XLA Ops:
  6.5 1.0 multiply_convert_fusion.1
  7.5 0.2 reshape.107
  7.7 0.2 copy.67
  7.9 0.8 reshape.115
  8.7 21.8 %all-to-all-start = ((bf16[64,2,512]{2,1,0:T(2,128)(2,1)}), bf16[64,2,512]{2,1,0:T(2,128)(2,1)S(1)}, u32[]{:S(2)}, u32[]{:S(2)}) async-start(bf16[64,2,512]{2,1,0:T(2,128)(2,1)} %reshape.115), calls=%async_computation | async-start | bytes 262144 | tf_op jit(solution)/shard_map/all_to_all | solution.py:17
  30.6 17.1 %all-to-all-done = bf16[64,2,512]{2,1,0:T(2,128)(2,1)S(1)} async-done(((bf16[64,2,512]{2,1,0:T(2,128)(2,1)}), bf16[64,2,512]{2,1,0:T(2,128)(2,1)S(1)}, u32[]{:S(2)}, u32[]{:S(2)}) %all-to-all-start) | async-done | bytes 131104 | tf_op jit(solution)/shard_map/all_to_all | solution.py:17
  47.7 0.2 reshape.116
  47.9 16.1 %fusion.7 = f32[1024,64]{0,1:T(8,128)S(1)} fusion(bf16[1024,64]{1,0:T(8,128)(2,1)S(1)} %bitcast.78), kind=kOutput, calls=%fused_computation.13 | convolution fusion | flops 149946368 | bytes 393216 | tf_op jit(solution)/shard_map/dot_general | solution.py:44
  64.0 0.0 copy-start
  64.0 17.0 %fusion.20 = (bf16[1,1024,64]{1,2,0:T(8,128)(2,1)S(1)}, bf16[1,1024,64]{1,2,0:T(8,128)(2,1)S(1)}) fusion(f32[1024,64]{0,1:T(8,128)S(1)} %fusion.7, s32[64]{0:T(128)S(1)} %and_select_fusion, bf16[1024,64]{1,0:T(8,128)(2,1)S(1)} %bitcast.79), kind=kOutput, calls=%fused_computation.49 | convolution fusion | flops 151453696 | bytes 655616 | tf_op jit(solution)/shard_map/dot_general | solution.py:45
  81.0 0.4 copy.46
  81.4 1.0 reshape.117
  82.4 4.5 %all-to-all-start.1 = ((bf16[64,2,1024]{2,1,0:T(2,128)(2,1)}), bf16[64,2,1024]{2,1,0:T(2,128)(2,1)S(1)}, u32[]{:S(2)}, u32[]{:S(2)}) async-start(bf16[64,2,1024]{2,1,0:T(2,128)(2,1)} %reshape.117), calls=%async_computation.1 | async-start | bytes 524288 | tf_op jit(solution)/shard_map/all_to_all | solution.py:21
  86.9 0.0 reduce-scatter.2.cloned.1.call-start
  87.0 0.1 cosine_multiply_fusion
  87.0 0.1 copy.51
  87.1 0.1 copy.52
  87.2 0.0 copy-done
  87.2 22.0 %all-to-all-done.1 = bf16[64,2,1024]{2,1,0:T(2,128)(2,1)S(1)} async-done(((bf16[64,2,1024]{2,1,0:T(2,128)(2,1)}), bf16[64,2,1024]{2,1,0:T(2,128)(2,1)S(1)}, u32[]{:S(2)}, u32[]{:S(2)}) %all-to-all-start.1) | async-done | bytes 262176 | tf_op jit(solution)/shard_map/all_to_all | solution.py:21
  109.2 0.3 reshape.118
  109.6 0.1 copy.47
  109.7 0.1 copy.48
  109.8 0.3 reshape.109
  110.1 0.3 convolution_bitcast_fusion.3
  110.4 0.3 convolution_bitcast_fusion.2
  110.7 0.4 subtract_convert_fusion.1
  111.1 0.3 convolution_bitcast_fusion.1
  111.3 0.3 convolution_bitcast_fusion
  111.6 0.2 subtract_convert_fusion
  111.7 0.2 stack.31
  111.9 0.2 copy.53
  112.1 0.2 stack.32
  112.3 0.2 copy.54
  112.4 0.1 fusion.78
  112.6 0.3 reshape.119
  112.9 26.4 %all_to_all.54 = bf16[64,2,1024]{2,1,0:T(2,128)(2,1)S(1)} all-to-all(bf16[64,2,1024]{2,1,0:T(2,128)(2,1)S(1)} %reshape.119), channel_id=1, replica_groups=mesh['seq'=64,'chan'=16] {'seq'}, dimensions={0} | all-to-all | bytes 524288 | tf_op jit(solution)/shard_map/all_to_all | solution.py:17
  139.3 0.3 reshape.120
  139.7 16.1 %fusion.6 = f32[1024,64]{0,1:T(8,128)S(1)} fusion(bf16[1024,64]{1,0:T(8,128)(2,1)S(1)} %bitcast.81), kind=kOutput, calls=%fused_computation.12 | convolution fusion | flops 149946368 | bytes 393216 | tf_op jit(solution)/shard_map/dot_general | solution.py:75
  155.8 16.2 %fusion.13 = bf16[1,1024,64]{1,2,0:T(8,128)(2,1)S(1)} fusion(f32[1024,64]{0,1:T(8,128)S(1)} %fusion.6, bf16[1024,64]{1,0:T(8,128)(2,1)S(1)} %bitcast.80), kind=kOutput, calls=%fused_computation.23 | convolution fusion | flops 150142976 | bytes 524288 | tf_op jit(solution)/shard_map/dot_general | solution.py:76
  171.9 0.0 copy-start.1
  171.9 0.4 copy.55
  172.3 0.5 broadcast.193
  172.8 2.3 reduce
  175.1 0.2 reshape.121
  175.3 21.1 %all_to_all.55 = bf16[64,2,512]{2,1,0:T(2,128)(2,1)S(1)} all-to-all(bf16[64,2,512]{2,1,0:T(2,128)(2,1)S(1)} %reshape.121), channel_id=1, replica_groups=mesh['seq'=64,'chan'=16] {'seq'}, dimensions={0} | all-to-all | bytes 262144 | tf_op jit(solution)/shard_map/all_to_all | solution.py:21
  196.4 0.3 reshape.122
  196.8 0.2 copy.57
  197.0 0.2 reshape.111
  197.2 0.0 copy-done.1
  197.2 5.4 %convolution_convert_fusion = bf16[256,8192]{1,0:T(8,128)(2,1)} fusion(bf16[256,8192]{1,0:T(8,128)(2,1)} %param.9, f32[256,256]{1,0:T(8,128)S(1)} %reshape.111, bf16[256,256]{1,0:T(8,128)(2,1)S(1)} %copy-done.1), kind=kOutput, calls=%fused_computation | convolution fusion | flops 1076035584 | bytes 8781824 | tf_op jit(solution)/shard_map/dot_general | solution.py:80
  202.6 0.0 reduce-scatter.2.cloned.1.call-update
  202.6 101.9 %reduce-scatter.2.cloned.1.call-done = bf16[256,512]{1,0:T(8,128)(2,1)} async-done(((bf16[256,8192]{1,0:T(8,128)(2,1)}), bf16[256,512]{1,0:T(8,128)(2,1)}) %reduce-scatter.2.cloned.1.call-update) | async-done | bytes 262160 | tf_op jit(solution)/shard_map/reduce_scatter | solution.py:81
  (8 shorter events, 0.2 us)
Async XLA Ops:
  8.7 38.9 %all-to-all-start = ((bf16[64,2,512]{2,1,0:T(2,128)(2,1)}), bf16[64,2,512]{2,1,0:T(2,128)(2,1)S(1)}, u32[]{:S(2)}, u32[]{:S(2)}) async-start(bf16[64,2,512]{2,1,0:T(2,128)(2,1)} %reshape.115), calls=%async_computation | async-start | bytes 262144 | tf_op jit(solution)/shard_map/all_to_all | solution.py:17
  64.0 23.2 %copy-start = (f32[2,16,16,256]{3,2,1,0:T(8,128)S(1)}, f32[2,16,16,256]{3,2,1,0:T(8,128)}, u32[]{:S(2)}) copy-start(f32[2,16,16,256]{3,2,1,0:T(8,128)} %param.8) | copy-start | bytes 1572868
  82.4 26.8 %all-to-all-start.1 = ((bf16[64,2,1024]{2,1,0:T(2,128)(2,1)}), bf16[64,2,1024]{2,1,0:T(2,128)(2,1)S(1)}, u32[]{:S(2)}, u32[]{:S(2)}) async-start(bf16[64,2,1024]{2,1,0:T(2,128)(2,1)} %reshape.117), calls=%async_computation.1 | async-start | bytes 524288 | tf_op jit(solution)/shard_map/all_to_all | solution.py:21
  86.9 217.7 %reduce-scatter.2.cloned.1.call-start = ((), (), s32[]{:S(2)}) async-start(), calls=%async_computation.5 | async-start | bytes 4456448 | tf_op jit(solution)/shard_map/reduce_scatter | solution.py:81
  171.9 25.3 %copy-start.1 = (bf16[256,256]{1,0:T(8,128)(2,1)S(1)}, bf16[256,256]{1,0:T(8,128)(2,1)}, u32[]{:S(2)}) copy-start(bf16[256,256]{1,0:T(8,128)(2,1)} %param.7) | copy-start | bytes 393220
Sparse Core Ops, SparseCore 0:
  202.7 101.7 reduce-scatter.1
where the time goes:
time: 316 us; the launch traced here: 312 us
  waiting for transfers between devices  141 us (45%)
  matrix products  71.7 us (23%)
  blocking collectives  47.5 us (15%)
  starting transfers between devices  26.3 us (8%)
  between operations  13.9 us (4%)
  local copies, waits for them, and re-layouts  7.03 us (2%)
  other arithmetic  4.09 us (1%)
    reduce_scatter x1, waiting for transfers between devices, shards(): lax.psum_scatter(partial_sum.astype(jnp.bfloat16), 'chan', scatter_dimens...  102 us
    all_to_all x1, blocking collectives, to_columns(): return lax.all_to_all(data, 'seq', split_axis=2, concat_axis=1, tiled=True)  26.4 us
    all_to_all x1, waiting for transfers between devices, to_rows(): return lax.all_to_all(data, 'seq', split_axis=1, concat_axis=2, tiled=True)  22 us
    all_to_all x1, starting transfers between devices, to_columns(): return lax.all_to_all(data, 'seq', split_axis=2, concat_axis=1, tiled=True)  21.8 us
    all_to_all x1, blocking collectives, to_rows(): return lax.all_to_all(data, 'seq', split_axis=1, concat_axis=2, tiled=True)  21.1 us
    all_to_all x1, waiting for transfers between devices, to_columns(): return lax.all_to_all(data, 'seq', split_axis=2, concat_axis=1, tiled=True)  17.1 us
    dot_general x1, matrix products, shards(): jnp.dot(jnp.transpose(block_sin), columns, preferred_element_type=jnp.flo...  17 us
    dot_general x1, matrix products, shards(): jnp.dot(block_sin, gathered[1], preferred_element_type=jnp.float32)  16.2 us
  transfers between devices with their start and end apart: 3, of which 3 were waited for; matrix products, arithmetic and copies ran while one was open for 0% of the time, Pallas kernels for 0%

commit v1 on v0

v1 whole, which is shorter than its diff:
```python
import functools
import math

import jax
import jax.numpy as jnp
import ml_dtypes
import numpy as np
from jax import lax
from jax.experimental import pallas as pl
from jax.experimental.pallas import tpu as pltpu
from jax.sharding import PartitionSpec as P

BLOCK = 1024
SPAN = 16
TOKENS = 16384
SEQ = 64
HALF = 8
LANES = 128
OWN = 4
MESH = pl.DeviceIdType.MESH
BF16 = jnp.bfloat16
F32 = jnp.float32


def tables():
    freq = np.arange(BLOCK)
    base = (16 * np.arange(SEQ)[:, None] + np.arange(HALF)[None, :]).reshape(-1)
    angle = 2.0 * math.pi * ((freq[:, None] * base[None, :]) % BLOCK) / BLOCK
    forward = np.concatenate([np.cos(angle), -np.sin(angle)]).astype(ml_dtypes.bfloat16)
    inverse = np.ascontiguousarray(forward.T)
    lane = np.arange(LANES)
    place = lane % SPAN + 128 * (lane // 64)
    turn = 2.0 * math.pi * ((freq[:, None] * place[None, :]) % TOKENS) / TOKENS
    twist = np.stack([np.cos(turn), -np.sin(turn)]).astype(np.float32)
    span = np.arange(SPAN)
    span_angle = 2.0 * math.pi * ((span[:, None] * span[None, :]) % SPAN) / SPAN
    cos, sin = np.cos(span_angle), np.sin(span_angle)
    same = np.eye(OWN)

    def spread(block):
        return np.kron(same, block)

    re_rows = [np.tile(spread(cos), (2, 1)), np.tile(spread(sin), (2, 1))]
    im_rows = [np.tile(-spread(sin), (2, 1)), np.tile(spread(cos), (2, 1))]
    re, im = np.concatenate(re_rows), np.concatenate(im_rows)
    mix = np.concatenate([re, re, -im, im], axis=1).astype(ml_dtypes.bfloat16)
    back_re = np.concatenate([spread(cos.T), -spread(sin.T)])
    back_im = np.concatenate([spread(sin.T), spread(cos.T)])
    unmix = np.concatenate([back_re, back_re, back_im, back_im], axis=1)
    unmix = (unmix.astype(ml_dtypes.bfloat16).astype(np.float32) / TOKENS).astype(ml_dtypes.bfloat16)
    chan = np.arange(SEQ * OWN)
    pick = (chan[None, :] // OWN == np.arange(SEQ)[:, None]).astype(ml_dtypes.bfloat16)
    pick_t = np.ascontiguousarray(pick.T)
    row = np.arange(2 * SPAN)
    fold = (row[:, None] // SPAN == lane[None, :] // 64) & (row[:, None] % SPAN == lane[None, :] % SPAN)
    fold = fold.astype(ml_dtypes.bfloat16)
    return forward, inverse, twist, mix, unmix, pick, pick_t, fold


def dot(left, right):
    return jnp.dot(left, right, preferred_element_type=F32)


def dot_t(left, right):
    return lax.dot_general(left, right, (((1,), (1,)), ((), ())), preferred_element_type=F32)


def conv_kernel(
    values_h, gate_in_h, gate_out_h, spectrum_h, forward_h, inverse_h, twist_h,
    mix_h, unmix_h, pick_h, pick_t_h, fold_h, out,
    values, gate_in, gate_out, spectrum, forward, inverse, twist, mix, unmix, pick, pick_t, fold,
    stage, tok_send, tok_recv, wide, spec_send, spec_recv, freq, turned, back_send, back_recv,
    load_sem, send_sem, recv_sem,
):
    me = lax.axis_index("seq")
    sources = (values_h, gate_in_h, pick_h, forward_h, twist_h, mix_h, unmix_h, inverse_h,
               gate_out_h, pick_t_h, fold_h)
    targets = (values, gate_in, pick, forward, twist, mix, unmix, inverse,
               gate_out, pick_t, fold)
    loads = [
        pltpu.make_async_copy(src, dst, load_sem.at[i]) for i, (src, dst) in enumerate(zip(sources, targets))
    ]
    halves = [
        pltpu.make_async_copy(
            spectrum_h.at[:, pl.ds(LANES * i, LANES)], spectrum.at[i], load_sem.at[len(loads) + i]
        )
        for i in range(2)
    ]
    for load in loads[:3] + halves + loads[3:]:
        load.start()
    barrier = pltpu.get_barrier_semaphore()

    @pl.loop(1, SEQ)
    def _(i):
        pl.semaphore_signal(
            barrier, inc=1, device_id={"seq": lax.rem(me + i, SEQ)}, device_id_type=MESH
        )

    def exchange(send, recv, slot):
        @pl.loop(1, SEQ)
        def _(i):
            peer = lax.rem(me + i, SEQ)
            pltpu.make_async_remote_copy(
                src_ref=send.at[peer], dst_ref=recv.at[me],
                send_sem=send_sem.at[slot], recv_sem=recv_sem.at[slot],
                device_id={"seq": peer}, device_id_type=MESH,
            ).start()

    def settled(ref, sem):
        part = ref.at[pl.ds(0, SEQ - 1)]
        pltpu.make_async_copy(part, part, sem).wait()

    lane = lax.broadcasted_iota(jnp.int32, (SPAN, SEQ * OWN), 1)
    masks = [lax.rem(lane, OWN) == h for h in range(OWN)]
    for load in loads[:3]:
        load.wait()
    picked = pick[...]
    for low in range(HALF):
        pieces = []
        for high in range(2):
            rows = pl.ds((high * HALF + low) * SPAN, SPAN)
            block = (values[rows, :].astype(F32) * gate_in[rows, :].astype(F32)).astype(BF16).astype(F32)
            pieces += [jnp.where(mask, block, 0.0) for mask in masks]
        spread = jnp.concatenate(pieces, axis=0).astype(BF16)
        stage[pl.ds(low, SEQ, stride=HALF), :] = dot_t(picked, spread)
    tok_send[...] = stage[...].reshape(SEQ, HALF, LANES).astype(BF16)
    pl.semaphore_wait(barrier, SEQ - 1)
    exchange(tok_send, tok_recv, 0)
    tok_recv[me] = tok_send[me]
    for load in halves:
        load.wait()
    for col in range(SPAN):
        rows = pl.ds(col, 2 * SPAN, stride=SPAN)
        block = jnp.concatenate([spectrum[0, rows, :], spectrum[1, rows, :]], axis=1)
        pieces = []
        for part in range(2):
            half = block[part * SPAN:(part + 1) * SPAN]
            pieces += [jnp.where(mask, half, 0.0) for mask in masks]
        spread = jnp.concatenate(pieces, axis=0).astype(BF16)
        wide[pl.ds(col, SEQ, stride=SPAN), :] = dot_t(picked, spread)
    spec_send[...] = wide[...].reshape(SEQ, SPAN, LANES).astype(BF16)
    exchange(spec_send, spec_recv, 1)
    spec_recv[me] = spec_send[me]
    for load in loads[3:]:
        load.wait()
    settled(tok_recv, recv_sem.at[0])
    columns = tok_recv[...].reshape(SEQ * HALF, LANES)
    step = 256

    @pl.loop(0, BLOCK // step)
    def _(i):
        rows = pl.ds(pl.multiple_of(i * step, step), step)
        im_rows = pl.ds(pl.multiple_of(BLOCK + i * step, step), step)
        re, im = dot(forward[rows, :], columns), dot(forward[im_rows, :], columns)
        tr, ti = twist[0, rows, :], twist[1, rows, :]
        pair = jnp.concatenate([re * tr - im * ti, re * ti + im * tr], axis=1).astype(BF16)
        freq[rows, :] = dot(pair, mix[...])

    settled(spec_recv, recv_sem.at[1])

    @pl.loop(0, BLOCK // step)
    def _(i):
        rows = pl.ds(pl.multiple_of(i * step, step), step)
        im_rows = pl.ds(pl.multiple_of(BLOCK + i * step, step), step)
        filt = spec_recv[pl.ds(i * (step // SPAN), step // SPAN)].reshape(step, LANES).astype(F32)
        prod = freq[rows, :LANES] * filt + freq[rows, LANES:] * pltpu.roll(filt, 64, 1)
        back = dot(prod.astype(BF16), unmix[...])
        re, im = back[:, :LANES], back[:, LANES:]
        tr, ti = twist[0, rows, :], twist[1, rows, :]
        turned[rows, :] = (re * tr + im * ti).astype(BF16)
        turned[im_rows, :] = (im * tr - re * ti).astype(BF16)

    @pl.loop(0, 4)
    def _(i):
        rows = pl.ds(pl.multiple_of(i * 128, 128), 128)
        conv = dot(inverse[rows, :], turned[...])
        back_send[pl.ds(i * 16, 16)] = conv.reshape(16, HALF, LANES).astype(BF16)

    exchange(back_send, back_recv, 2)
    back_recv[me] = back_send[me]
    settled(back_recv, recv_sem.at[2])
    stage[...] = back_recv[...].reshape(SEQ * HALF, LANES).astype(F32)
    chan_row = lax.rem(lax.broadcasted_iota(jnp.int32, (SEQ * OWN, LANES), 0), OWN)
    chan_lane = lax.rem(lax.broadcasted_iota(jnp.int32, (SEQ * OWN, LANES), 1) // SPAN, OWN)
    for low in range(HALF):
        block = stage[pl.ds(low, SEQ, stride=HALF), :].astype(BF16)
        spread = jnp.where(chan_row == chan_lane, dot(pick_t[...], block), 0.0).astype(BF16)
        conv = dot_t(fold[...], spread)
        for high in range(2):
            rows = pl.ds((high * HALF + low) * SPAN, SPAN)
            gate = gate_out[rows, :].astype(F32)
            out[rows, :] = (conv[high * SPAN:(high + 1) * SPAN] * gate).astype(BF16)
    settled(tok_send, send_sem.at[0])
    settled(spec_send, send_sem.at[1])
    settled(back_send, send_sem.at[2])


def convolve(values, gate_in, gate_out, spectrum):
    forward, inverse, twist, mix, unmix, pick, pick_t, fold = tables()
    rows, width = values.shape
    flat = spectrum.reshape(2 * SPAN * SPAN, width)
    loaded = [(values.shape, BF16)] * 3 + [((2, 2 * SPAN * SPAN, LANES), F32)]
    loaded += [(t.shape, F32 if t.dtype == np.float32 else BF16) for t in
               (forward, inverse, twist, mix, unmix, pick, pick_t, fold)]
    scratch = [pltpu.VMEM(shape, dtype) for shape, dtype in loaded]
    scratch += [
        pltpu.VMEM((SEQ * HALF, LANES), F32),
        pltpu.VMEM((SEQ, HALF, LANES), BF16),
        pltpu.VMEM((SEQ, HALF, LANES), BF16),
        pltpu.VMEM((SEQ * SPAN, LANES), F32),
        pltpu.VMEM((SEQ, SPAN, LANES), BF16),
        pltpu.VMEM((SEQ, SPAN, LANES), BF16),
        pltpu.VMEM((BLOCK, 2 * LANES), F32),
        pltpu.VMEM((2 * BLOCK, LANES), BF16),
        pltpu.VMEM((SEQ, HALF, LANES), BF16),
        pltpu.VMEM((SEQ, HALF, LANES), BF16),
        pltpu.SemaphoreType.DMA((len(loaded) + 1,)),
        pltpu.SemaphoreType.DMA((3,)),
        pltpu.SemaphoreType.DMA((3,)),
    ]
    return pl.pallas_call(
        conv_kernel,
        out_shape=jax.ShapeDtypeStruct((rows, width), BF16),
        in_specs=[pl.BlockSpec(memory_space=pl.ANY)] * 12,
        out_specs=pl.BlockSpec(memory_space=pltpu.VMEM),
        scratch_shapes=scratch,
        compiler_params=pltpu.CompilerParams(
            collective_id=0, has_side_effects=True, vmem_limit_bytes=40 << 20
        ),
        name="convolve",
    )(values, gate_in, gate_out, flat, *[jnp.asarray(t) for t in
      (forward, inverse, twist, mix, unmix, pick, pick_t, fold)])


def shards(values, gate_in, gate_out, spectrum, out_weight):
    gated = convolve(values, gate_in, gate_out, spectrum)
    partial_sum = jnp.dot(gated, out_weight, preferred_element_type=F32)
    return lax.psum_scatter(partial_sum.astype(BF16), "chan", scatter_dimension=1, tiled=True)


def solution(mesh):
    placed = (
        P("seq", "chan"),
        P("seq", "chan"),
        P("seq", "chan"),
        P(None, None, "seq", "chan"),
        P("chan", None),
    )
    return jax.shard_map(
        shards, mesh=mesh, in_specs=placed, out_specs=P("seq", "chan"), check_vma=False
    )
```

time: 316 us -> 194 us (0.61); the launches traced: 312 us -> 193 us
  matrix products: 71.7 us -> 3.21 us
  Pallas kernels: 0 us -> 60.4 us
  blocking collectives: 47.5 us -> 0 us
  waiting for transfers between devices: 141 us -> 104 us
  starting transfers between devices: 26.3 us -> 0.01 us
  local copies, waits for them, and re-layouts: 7.03 us -> 12.2 us
  other arithmetic: 4.09 us -> 0 us
    dot_general x9 -> x1, matrix products: 71.7 us -> 3.21 us  [shards(): partial_sum = jnp.dot(gated, out_weight, preferred_element_type=F32)]
    pallas_call x0 -> x1, Pallas kernels: none -> 60.4 us  [convolve(): pl.pallas_call(conv_kernel, out_shape=jax.ShapeDtypeStruct((rows, width),...]
    all_to_all x2 -> x0, blocking collectives: 47.5 us -> none  [the longest x1 26.4 us: to_columns(): return lax.all_to_all(data, 'seq', split_axis=2, concat_axis=1, tiled=True)]
    all_to_all x2 -> x0, waiting for transfers between devices: 39.1 us -> none  [the longest x1 22 us: to_rows(): return lax.all_to_all(data, 'seq', split_axis=1, concat_axis=2, tiled=True)]
    all_to_all x2 -> x0, starting transfers between devices: 26.3 us -> none  [the longest x1 21.8 us: to_columns(): return lax.all_to_all(data, 'seq', split_axis=2, concat_axis=1, tiled=True)]
    unnamed x13 -> x26, local copies, waits for them, and re-layouts: 4.08 us -> 12.2 us
  transfers between devices with their start and end apart: 3 -> 1, of which waited for: 3 -> 1; matrix products, arithmetic and copies ran while one was open for 0% -> 0% of each run, Pallas kernels for 0% -> 0%
where the time goes in v1:
time: 194 us; the launch traced here: 193 us
  waiting for transfers between devices  104 us (54%)
  Pallas kernels  60.4 us (31%)
  between operations  13.4 us (7%)
  local copies, waits for them, and re-layouts  12.2 us (6%)
  matrix products  3.21 us (2%)
    reduce_scatter x1, waiting for transfers between devices, shards(): lax.psum_scatter(partial_sum.astype(BF16), 'chan', scatter_dimension=1, t...  104 us
    pallas_call x1, Pallas kernels, convolve(): pl.pallas_call(conv_kernel, out_shape=jax.ShapeDtypeStruct((rows, width),...  60.4 us
    unnamed x26, local copies, waits for them, and re-layouts  12.2 us
  transfers between devices with their start and end apart: 1, of which 1 were waited for; matrix products, arithmetic and copies ran while one was open for 0% of the time, Pallas kernels for 0%

profile of v1, /device:TPU:1, one launch (start us, length us, event | category | flops | bytes accessed | tf_op | source)
XLA Modules:
  0.0 193.3 jit_solution(413073139333662381)
XLA Ops:
  6.5 0.0 reduce-scatter.2.cloned.1.call-start
  6.5 0.0 copy-start
  6.5 1.6 copy-done
  8.1 0.0 copy-start.1
  8.1 1.6 copy-done.1
  9.7 0.0 copy-start.2
  9.7 1.2 copy-done.2
  10.9 0.0 copy-start.3
  10.9 1.0 copy-done.3
  12.0 0.0 copy-start.4
  12.0 0.9 copy-done.4
  12.9 0.0 copy-start.5
  12.9 0.9 copy-done.5
  13.8 0.0 copy-start.6
  13.8 0.9 copy-done.6
  14.7 0.0 copy-start.7
  14.7 0.9 copy-done.7
  15.6 0.0 copy-start.8
  15.6 0.8 copy-done.8
  16.4 0.0 copy-start.9
  16.4 0.8 copy-done.9
  17.3 0.0 copy-start.10
  17.3 0.8 copy-done.10
  18.0 0.0 copy-start.11
  18.0 0.7 copy-done.11
  18.7 0.0 copy-start.12
  18.7 60.4 %convolve.1 = bf16[256,256]{1,0:T(8,128)(2,1)S(1)} custom-call(bf16[256,256]{1,0:T(8,128)(2,1)S(1)} %copy-done.4, bf16[256,256]{1,0:T(8,128)(2,1)S(1)} %copy-done.5, bf16[256,256]{1,0:T(8,128)(2,1)S(1)} %copy-done.6, f32[512,256]{1,0:T(8,128)S(1)} %bitcast.3, bf16[2048,512]{1,0:T(8,128)(2,1)S(1)} %copy-done.1, bf16[512,2048]{1,0:T(8,128)(2,1)S(1)} %copy-done, ...), custom_call_target="tpu_custom_call" | custom-call | tf_op jit(solution)/shard_map/convolve/pallas_call | solution.py:221
  79.2 0.0 copy-done.12
  79.2 3.2 %convolution_convert_fusion = bf16[256,8192]{1,0:T(8,128)(2,1)} fusion(bf16[256,256]{1,0:T(8,128)(2,1)S(1)} %convolve.1, bf16[256,8192]{1,0:T(8,128)(2,1)S(1)} %copy-done.12), kind=kOutput, calls=%fused_computation | convolution fusion | flops 1075838976 | bytes 8519680 | tf_op jit(solution)/shard_map/dot_general | solution.py:237
  82.4 0.0 reduce-scatter.2.cloned.1.call-update
  82.4 104.1 %reduce-scatter.2.cloned.1.call-done = bf16[256,512]{1,0:T(8,128)(2,1)} async-done(((bf16[256,8192]{1,0:T(8,128)(2,1)}), bf16[256,512]{1,0:T(8,128)(2,1)}) %reduce-scatter.2.cloned.1.call-update) | async-done | bytes 262160 | tf_op jit(solution)/shard_map/reduce_scatter | solution.py:238
Async XLA Ops:
  6.5 179.9 %reduce-scatter.2.cloned.1.call-start = ((), (), s32[]{:S(2)}) async-start(), calls=%async_computation.1 | async-start | bytes 4456448 | tf_op jit(solution)/shard_map/reduce_scatter | solution.py:238
  6.5 1.6 copy-start
  8.1 1.6 copy-start.1
  9.7 1.2 copy-start.2
  10.9 1.0 copy-start.3
  12.0 0.9 copy-start.4
  12.9 0.9 copy-start.5
  13.8 0.9 copy-start.6
  14.7 0.9 copy-start.7
  15.6 0.8 copy-start.8
  16.4 0.8 copy-start.9
  17.3 0.8 copy-start.10
  18.0 0.7 copy-start.11
  18.7 60.4 %copy-start.12 = (bf16[256,8192]{1,0:T(8,128)(2,1)S(1)}, bf16[256,8192]{1,0:T(8,128)(2,1)}, u32[]{:S(2)}) copy-start(bf16[256,8192]{1,0:T(8,128)(2,1)} %param.17) | copy-start | bytes 12582916
Sparse Core Ops, SparseCore 0:
  82.5 103.9 reduce-scatter.1

commit v2 on v1

--- a/solution.py
+++ b/solution.py
@@ -16,6 +16,7 @@
 SEQ = 64
 HALF = 8
 LANES = 128
+SIDE = 4
 OWN = 4
 MESH = pl.DeviceIdType.MESH
 BF16 = jnp.bfloat16
@@ -65,14 +66,19 @@
     return lax.dot_general(left, right, (((1,), (1,)), ((), ())), preferred_element_type=F32)
 
 
-def conv_kernel(
-    values_h, gate_in_h, gate_out_h, spectrum_h, forward_h, inverse_h, twist_h,
+def layer_kernel(
+    values_h, gate_in_h, gate_out_h, spectrum_h, weight_h, forward_h, inverse_h, twist_h,
     mix_h, unmix_h, pick_h, pick_t_h, fold_h, out,
     values, gate_in, gate_out, spectrum, forward, inverse, twist, mix, unmix, pick, pick_t, fold,
     stage, tok_send, tok_recv, wide, spec_send, spec_recv, freq, turned, back_send, back_recv,
-    load_sem, send_sem, recv_sem,
+    weight, gated, total, part_send, part_recv,
+    load_sem, send_sem, recv_sem, weight_sem, pair_sem, gated_sem, part_sem,
 ):
     me = lax.axis_index("seq")
+    group = lax.axis_index("chan")
+    col_x, col_y = lax.rem(group, SIDE), group // SIDE
+    core = lax.rem(me, 2)
+    sibling = me + 1 - 2 * core
     sources = (values_h, gate_in_h, pick_h, forward_h, twist_h, mix_h, unmix_h, inverse_h,
                gate_out_h, pick_t_h, fold_h)
     targets = (values, gate_in, pick, forward, twist, mix, unmix, inverse,
@@ -88,6 +94,18 @@
     ]
     for load in loads[:3] + halves + loads[3:]:
         load.start()
+    half_k, cols_each = weight.shape[1] // (2 * SIDE), weight.shape[2]
+
+    def own_weight(i):
+        cols = pl.multiple_of((i * SIDE + col_x) * cols_each, cols_each)
+        rows = pl.multiple_of(col_x * 2 * half_k, 2 * half_k)
+        return pltpu.make_async_copy(
+            weight_h.at[:, pl.ds(cols, cols_each)], weight.at[i, pl.ds(rows, 2 * half_k), :],
+            load_sem.at[len(loads) + 2 + i],
+        )
+
+    for i in range(SIDE):
+        own_weight(i).start()
     barrier = pltpu.get_barrier_semaphore()
 
     @pl.loop(1, SEQ)
@@ -95,6 +113,16 @@
         pl.semaphore_signal(
             barrier, inc=1, device_id={"seq": lax.rem(me + i, SEQ)}, device_id_type=MESH
         )
+
+    def at_x(i):
+        return col_y * SIDE + lax.rem(col_x + i, SIDE)
+
+    def at_y(i):
+        return lax.rem(col_y + i, SIDE) * SIDE + col_x
+
+    for i in range(1, SIDE):
+        for peer in (at_x(i), at_y(i)):
+            pl.semaphore_signal(barrier, inc=1, device_id={"chan": peer}, device_id_type=MESH)
 
     def exchange(send, recv, slot):
         @pl.loop(1, SEQ)
@@ -124,9 +152,22 @@
         spread = jnp.concatenate(pieces, axis=0).astype(BF16)
         stage[pl.ds(low, SEQ, stride=HALF), :] = dot_t(picked, spread)
     tok_send[...] = stage[...].reshape(SEQ, HALF, LANES).astype(BF16)
-    pl.semaphore_wait(barrier, SEQ - 1)
+    pl.semaphore_wait(barrier, SEQ - 1 + 2 * (SIDE - 1))
     exchange(tok_send, tok_recv, 0)
     tok_recv[me] = tok_send[me]
+    half_rows = pl.multiple_of(core * half_k, half_k)
+
+    @pl.loop(0, SIDE)
+    def _(i):
+        for j in range(1, SIDE):
+            cols = pl.multiple_of((i * SIDE + lax.rem(col_x + j, SIDE)) * cols_each, cols_each)
+            rows = pl.multiple_of(col_x * 2 * half_k + half_rows, half_k)
+            pltpu.make_async_remote_copy(
+                src_ref=weight_h.at[pl.ds(half_rows, half_k), pl.ds(cols, cols_each)],
+                dst_ref=weight.at[i, pl.ds(rows, half_k), :],
+                send_sem=weight_sem.at[SIDE], recv_sem=weight_sem.at[col_x],
+                device_id={"chan": at_x(j)}, device_id_type=MESH,
+            ).start()
     for load in halves:
         load.wait()
     for col in range(SPAN):
@@ -178,10 +219,26 @@
 
     exchange(back_send, back_recv, 2)
     back_recv[me] = back_send[me]
+
+    def weight_half(source, which):
+        rows = pl.multiple_of(source * 2 * half_k + which * half_k, half_k)
+        return weight.at[:, pl.ds(rows, half_k), :]
+
+    for i in (1, 3, 2):
+        source = lax.rem(col_x + i, SIDE)
+        mine = weight_half(source, core)
+        pltpu.make_async_copy(mine, mine, weight_sem.at[source]).wait()
+        pltpu.make_async_remote_copy(
+            src_ref=mine, dst_ref=mine, send_sem=pair_sem.at[SIDE], recv_sem=pair_sem.at[source],
+            device_id={"seq": sibling}, device_id_type=MESH,
+        ).start()
+
     settled(back_recv, recv_sem.at[2])
     stage[...] = back_recv[...].reshape(SEQ * HALF, LANES).astype(F32)
     chan_row = lax.rem(lax.broadcasted_iota(jnp.int32, (SEQ * OWN, LANES), 0), OWN)
     chan_lane = lax.rem(lax.broadcasted_iota(jnp.int32, (SEQ * OWN, LANES), 1) // SPAN, OWN)
+    width = SEQ * OWN
+    own_cols = pl.ds(pl.multiple_of(col_x * width, width), width)
     for low in range(HALF):
         block = stage[pl.ds(low, SEQ, stride=HALF), :].astype(BF16)
         spread = jnp.where(chan_row == chan_lane, dot(pick_t[...], block), 0.0).astype(BF16)
@@ -189,15 +246,59 @@
         for high in range(2):
             rows = pl.ds((high * HALF + low) * SPAN, SPAN)
             gate = gate_out[rows, :].astype(F32)
-            out[rows, :] = (conv[high * SPAN:(high + 1) * SPAN] * gate).astype(BF16)
+            gated[rows, own_cols] = (conv[high * SPAN:(high + 1) * SPAN] * gate).astype(BF16)
+    for i in (2, 1, 3):
+        pltpu.make_async_remote_copy(
+            src_ref=gated.at[:, own_cols], dst_ref=gated.at[:, own_cols],
+            send_sem=gated_sem.at[SIDE], recv_sem=gated_sem.at[col_x],
+            device_id={"chan": at_x(i)}, device_id_type=MESH,
+        ).start()
+    for i in range(SIDE):
+        own_weight(i).wait()
+    for i in (1, 3, 2):
+        source = lax.rem(col_x + i, SIDE)
+        other = weight_half(source, 1 - core)
+        pltpu.make_async_copy(other, other, pair_sem.at[source]).wait()
+    for i in (1, 3, 2):
+        source = lax.rem(col_x + i, SIDE)
+        cols = gated.at[:, pl.ds(pl.multiple_of(source * width, width), width)]
+        pltpu.make_async_copy(cols, cols, gated_sem.at[source]).wait()
+    for i in (2, 1, 3, 0):
+        target = lax.rem(col_y + i, SIDE)
+        for half in range(2):
+            cols = pl.ds(half * cols_each // 2, cols_each // 2)
+            part = dot(gated[...], weight[target, :, cols])
+            if i:
+                part_send[target, :, cols] = part.astype(BF16)
+            else:
+                total[:, cols] = part
+        if i:
+            pltpu.make_async_remote_copy(
+                src_ref=part_send.at[target], dst_ref=part_recv.at[col_y],
+                send_sem=part_sem.at[SIDE], recv_sem=part_sem.at[col_y],
+                device_id={"chan": at_y(i)}, device_id_type=MESH,
+            ).start()
+    for i in (1, 3, 2):
+        source = lax.rem(col_y + i, SIDE)
+        pltpu.make_async_copy(part_recv.at[source], part_recv.at[source], part_sem.at[source]).wait()
+        total[...] += part_recv[source].astype(F32)
+    out[...] = total[...].astype(BF16)
     settled(tok_send, send_sem.at[0])
     settled(spec_send, send_sem.at[1])
     settled(back_send, send_sem.at[2])
-
-
-def convolve(values, gate_in, gate_out, spectrum):
+    three = weight.at[:, pl.ds(0, 3 * half_k), :]
+    pltpu.make_async_copy(three, three, weight_sem.at[SIDE]).wait()
+    pltpu.make_async_copy(three, three, pair_sem.at[SIDE]).wait()
+    sent = gated.at[:, pl.ds(0, 3 * width)]
+    pltpu.make_async_copy(sent, sent, gated_sem.at[SIDE]).wait()
+    sent = part_send.at[pl.ds(0, 3)]
+    pltpu.make_async_copy(sent, sent, part_sem.at[SIDE]).wait()
+
+
+def layer(values, gate_in, gate_out, spectrum, out_weight):
     forward, inverse, twist, mix, unmix, pick, pick_t, fold = tables()
     rows, width = values.shape
+    cols_each = out_weight.shape[1] // (SIDE * SIDE)
     flat = spectrum.reshape(2 * SPAN * SPAN, width)
     loaded = [(values.shape, BF16)] * 3 + [((2, 2 * SPAN * SPAN, LANES), F32)]
     loaded += [(t.shape, F32 if t.dtype == np.float32 else BF16) for t in
@@ -214,28 +315,31 @@
         pltpu.VMEM((2 * BLOCK, LANES), BF16),
         pltpu.VMEM((SEQ, HALF, LANES), BF16),
         pltpu.VMEM((SEQ, HALF, LANES), BF16),
-        pltpu.SemaphoreType.DMA((len(loaded) + 1,)),
+        pltpu.VMEM((SIDE, SIDE * width, cols_each), BF16),
+        pltpu.VMEM((rows, SIDE * width), BF16),
+        pltpu.VMEM((rows, cols_each), F32),
+        pltpu.VMEM((SIDE, rows, cols_each), BF16),
+        pltpu.VMEM((SIDE, rows, cols_each), BF16),
+        pltpu.SemaphoreType.DMA((len(loaded) + 1 + SIDE,)),
         pltpu.SemaphoreType.DMA((3,)),
         pltpu.SemaphoreType.DMA((3,)),
+        pltpu.SemaphoreType.DMA((SIDE + 1,)),
+        pltpu.SemaphoreType.DMA((SIDE + 1,)),
+        pltpu.SemaphoreType.DMA((SIDE + 1,)),
+        pltpu.SemaphoreType.DMA((SIDE + 1,)),
     ]
     return pl.pallas_call(
-        conv_kernel,
-        out_shape=jax.ShapeDtypeStruct((rows, width), BF16),
-        in_specs=[pl.BlockSpec(memory_space=pl.ANY)] * 12,
+        layer_kernel,
+        out_shape=jax.ShapeDtypeStruct((rows, cols_each), BF16),
+        in_specs=[pl.BlockSpec(memory_space=pltpu.HBM)] * 13,
         out_specs=pl.BlockSpec(memory_space=pltpu.VMEM),
         scratch_shapes=scratch,
         compiler_params=pltpu.CompilerParams(
-            collective_id=0, has_side_effects=True, vmem_limit_bytes=40 << 20
+            collective_id=0, has_side_effects=True, vmem_limit_bytes=60 << 20
         ),
-        name="convolve",
-    )(values, gate_in, gate_out, flat, *[jnp.asarray(t) for t in
+        name="layer",
+    )(values, gate_in, gate_out, flat, out_weight, *[jnp.asarray(t) for t in
       (forward, inverse, twist, mix, unmix, pick, pick_t, fold)])
-
-
-def shards(values, gate_in, gate_out, spectrum, out_weight):
-    gated = convolve(values, gate_in, gate_out, spectrum)
-    partial_sum = jnp.dot(gated, out_weight, preferred_element_type=F32)
-    return lax.psum_scatter(partial_sum.astype(BF16), "chan", scatter_dimension=1, tiled=True)
 
 
 def solution(mesh):
@@ -247,5 +351,5 @@
         P("chan", None),
     )
     return jax.shard_map(
-        shards, mesh=mesh, in_specs=placed, out_specs=P("seq", "chan"), check_vma=False
+        layer, mesh=mesh, in_specs=placed, out_specs=P("seq", "chan"), check_vma=False
     )

time: 194 us -> 97.1 us (0.50)
  waiting for transfers between devices: 104 us -> 0 us
  Pallas kernels: 60.4 us -> 94.5 us
  between operations: 13.4 us -> 0.01 us
  local copies, waits for them, and re-layouts: 12.2 us -> 1.67 us
  matrix products: 3.21 us -> 0 us
    reduce_scatter x1 -> x0, waiting for transfers between devices: 104 us -> none  [shards(): lax.psum_scatter(partial_sum.astype(BF16), 'chan', scatter_dimension=1, t...]
    pallas_call x1, Pallas kernels: 60.4 us -> 94.5 us  [layer(): pl.pallas_call(layer_kernel, out_shape=jax.ShapeDtypeStruct((rows, cols_e...]
    unnamed x26 -> x1, local copies, waits for them, and re-layouts: 12.2 us -> 1.67 us
    dot_general x1 -> x0, matrix products: 3.21 us -> none  [shards(): partial_sum = jnp.dot(gated, out_weight, preferred_element_type=F32)]
  transfers between devices with their start and end apart: 1 -> 0, of which waited for: 1 -> 0; matrix products, arithmetic and copies ran while one was open for 0% -> 0% of each run, Pallas kernels for 0% -> 0%
where the time goes in v2:
time: 97.1 us; the launch traced here: 96.1 us
  Pallas kernels  94.5 us (97%)
  local copies, waits for them, and re-layouts  1.67 us (2%)
    pallas_call x1, Pallas kernels, layer(): pl.pallas_call(layer_kernel, out_shape=jax.ShapeDtypeStruct((rows, cols_e...  94.5 us

profile of v2, /device:TPU:1, one launch (start us, length us, event | category | flops | bytes accessed | tf_op | source)
XLA Modules:
  0.0 96.1 jit_solution(16981995969779739426)
XLA Ops:
  0.0 94.5 %layer.1 = bf16[256,512]{1,0:T(8,128)(2,1)} custom-call(bf16[256,256]{1,0:T(8,128)(2,1)} %values_h.1, bf16[256,256]{1,0:T(8,128)(2,1)} %gate_in_h.1, bf16[256,256]{1,0:T(8,128)(2,1)} %gate_out_h.1, f32[512,256]{1,0:T(8,128)} %bitcast.1, bf16[256,8192]{1,0:T(8,128)(2,1)} %weight_h.1, bf16[2048,512]{1,0:T(8,128)(2,1)} %constant.16.clone.forward_h, ...), custom_call_target="tpu_custom_call" | custom-call | tf_op jit(solution)/shard_map/layer/pallas_call | solution.py:331
  94.5 1.7 %copy.15 = bf16[256,512]{1,0:T(8,128)(2,1)} copy(bf16[256,512]{1,0:T(8,128)(2,1)} %layer.1) | data formatting | bytes 524288

commit v3 on v2

--- a/solution.py
+++ b/solution.py
@@ -18,6 +18,7 @@
 LANES = 128
 SIDE = 4
 OWN = 4
+FAR, DIRECT, MERGED = range(3)
 MESH = pl.DeviceIdType.MESH
 BF16 = jnp.bfloat16
 F32 = jnp.float32
@@ -71,7 +72,7 @@
     mix_h, unmix_h, pick_h, pick_t_h, fold_h, out,
     values, gate_in, gate_out, spectrum, forward, inverse, twist, mix, unmix, pick, pick_t, fold,
     stage, tok_send, tok_recv, wide, spec_send, spec_recv, freq, turned, back_send, back_recv,
-    weight, gated, total, part_send, part_recv,
+    weight, gated, total, kept, part_send, part_recv,
     load_sem, send_sem, recv_sem, weight_sem, pair_sem, gated_sem, part_sem,
 ):
     me = lax.axis_index("seq")
@@ -125,9 +126,10 @@
             pl.semaphore_signal(barrier, inc=1, device_id={"chan": peer}, device_id_type=MESH)
 
     def exchange(send, recv, slot):
-        @pl.loop(1, SEQ)
+        @pl.loop(0, SEQ - 1)
         def _(i):
-            peer = lax.rem(me + i, SEQ)
+            away = SEQ // 2 + ((i + 1) // 2) * (1 - 2 * lax.rem(i, 2))
+            peer = lax.rem(me + away, SEQ)
             pltpu.make_async_remote_copy(
                 src_ref=send.at[peer], dst_ref=recv.at[me],
                 send_sem=send_sem.at[slot], recv_sem=recv_sem.at[slot],
@@ -211,13 +213,21 @@
         turned[rows, :] = (re * tr + im * ti).astype(BF16)
         turned[im_rows, :] = (im * tr - re * ti).astype(BF16)
 
-    @pl.loop(0, 4)
-    def _(i):
-        rows = pl.ds(pl.multiple_of(i * 128, 128), 128)
+    for turn in (2, 1, 3, 0):
+        first = lax.rem(me // 16 + turn, 4) * 16
+        rows = pl.ds(pl.multiple_of(first * HALF, 128), 128)
         conv = dot(inverse[rows, :], turned[...])
-        back_send[pl.ds(i * 16, 16)] = conv.reshape(16, HALF, LANES).astype(BF16)
-
-    exchange(back_send, back_recv, 2)
+        back_send[pl.ds(first, 16)] = conv.reshape(16, HALF, LANES).astype(BF16)
+
+        @pl.loop(0 if turn else 1, 16)
+        def _(i):
+            peer = first + lax.rem(me + i, 16)
+            pltpu.make_async_remote_copy(
+                src_ref=back_send.at[peer], dst_ref=back_recv.at[me],
+                send_sem=send_sem.at[2], recv_sem=recv_sem.at[2],
+                device_id={"seq": peer}, device_id_type=MESH,
+            ).start()
+
     back_recv[me] = back_send[me]
 
     def weight_half(source, which):
@@ -239,60 +249,95 @@
     chan_lane = lax.rem(lax.broadcasted_iota(jnp.int32, (SEQ * OWN, LANES), 1) // SPAN, OWN)
     width = SEQ * OWN
     own_cols = pl.ds(pl.multiple_of(col_x * width, width), width)
+    chunk = part_send.shape[3]
+
+    def gated_part(step, source):
+        cols = pl.ds(pl.multiple_of(source * width, width), width)
+        return gated.at[pl.ds(step * chunk, chunk), cols]
+
     for low in range(HALF):
         block = stage[pl.ds(low, SEQ, stride=HALF), :].astype(BF16)
         spread = jnp.where(chan_row == chan_lane, dot(pick_t[...], block), 0.0).astype(BF16)
         conv = dot_t(fold[...], spread)
-        for high in range(2):
-            rows = pl.ds((high * HALF + low) * SPAN, SPAN)
-            gate = gate_out[rows, :].astype(F32)
-            gated[rows, own_cols] = (conv[high * SPAN:(high + 1) * SPAN] * gate).astype(BF16)
-    for i in (2, 1, 3):
-        pltpu.make_async_remote_copy(
-            src_ref=gated.at[:, own_cols], dst_ref=gated.at[:, own_cols],
-            send_sem=gated_sem.at[SIDE], recv_sem=gated_sem.at[col_x],
-            device_id={"chan": at_x(i)}, device_id_type=MESH,
-        ).start()
+        gate = jnp.concatenate(
+            [gate_out[pl.ds((high * HALF + low) * SPAN, SPAN), :] for high in range(2)], axis=0
+        ).astype(F32)
+        gated[pl.ds(low * 2 * SPAN, 2 * SPAN), own_cols] = (conv * gate).astype(BF16)
+        step, done = divmod(low + 1, HALF // 2)
+        if done == 0:
+            for i in (2, 1, 3):
+                pltpu.make_async_remote_copy(
+                    src_ref=gated_part(step - 1, col_x), dst_ref=gated_part(step - 1, col_x),
+                    send_sem=gated_sem.at[step - 1, SIDE], recv_sem=gated_sem.at[step - 1, col_x],
+                    device_id={"chan": at_x(i)}, device_id_type=MESH,
+                ).start()
     for i in range(SIDE):
         own_weight(i).wait()
     for i in (1, 3, 2):
         source = lax.rem(col_x + i, SIDE)
         other = weight_half(source, 1 - core)
         pltpu.make_async_copy(other, other, pair_sem.at[source]).wait()
-    for i in (1, 3, 2):
-        source = lax.rem(col_x + i, SIDE)
-        cols = gated.at[:, pl.ds(pl.multiple_of(source * width, width), width)]
-        pltpu.make_async_copy(cols, cols, gated_sem.at[source]).wait()
-    for i in (2, 1, 3, 0):
-        target = lax.rem(col_y + i, SIDE)
+
+    def pass_on(kind, step, way):
+        pltpu.make_async_remote_copy(
+            src_ref=part_send.at[kind, step, way], dst_ref=part_recv.at[kind, step, way],
+            send_sem=part_sem.at[3, 0, 0], recv_sem=part_sem.at[kind, step, way],
+            device_id={"chan": at_y(1 if way == 0 else 3)}, device_id_type=MESH,
+        ).start()
+
+    def arrived(kind, step, way):
+        ref = part_recv.at[kind, step, way]
+        pltpu.make_async_copy(ref, ref, part_sem.at[kind, step, way]).wait()
+        return ref[...].astype(F32)
+
+    half_cols = cols_each // 2
+    for step in range(2):
+        for i in (1, 3, 2):
+            part = gated_part(step, lax.rem(col_x + i, SIDE))
+            pltpu.make_async_copy(part, part, gated_sem.at[step, lax.rem(col_x + i, SIDE)]).wait()
+        rows = pl.ds(step * chunk, chunk)
+
+        def block_half(away, half):
+            target = lax.rem(col_y + away, SIDE)
+            return dot(gated[rows, :], weight[target, :, pl.ds(half * half_cols, half_cols)])
+
+        for way in range(2):
+            part_send[FAR, step, way] = block_half(2, way).astype(BF16)
+            pass_on(FAR, step, way)
+        for way, away in ((0, 1), (1, 3)):
+            part_send[DIRECT, step, way] = block_half(away, 1 - way).astype(BF16)
+            pass_on(DIRECT, step, way)
+        for way, away in ((0, 1), (1, 3)):
+            kept[step, way] = block_half(away, way)
         for half in range(2):
-            cols = pl.ds(half * cols_each // 2, cols_each // 2)
-            part = dot(gated[...], weight[target, :, cols])
-            if i:
-                part_send[target, :, cols] = part.astype(BF16)
-            else:
-                total[:, cols] = part
-        if i:
-            pltpu.make_async_remote_copy(
-                src_ref=part_send.at[target], dst_ref=part_recv.at[col_y],
-                send_sem=part_sem.at[SIDE], recv_sem=part_sem.at[col_y],
-                device_id={"chan": at_y(i)}, device_id_type=MESH,
-            ).start()
-    for i in (1, 3, 2):
-        source = lax.rem(col_y + i, SIDE)
-        pltpu.make_async_copy(part_recv.at[source], part_recv.at[source], part_sem.at[source]).wait()
-        total[...] += part_recv[source].astype(F32)
-    out[...] = total[...].astype(BF16)
+            total[rows, pl.ds(half * half_cols, half_cols)] = block_half(0, half)
+    for step in range(2):
+        for way in range(2):
+            part_send[MERGED, step, way] = (kept[step, way] + arrived(FAR, step, way)).astype(BF16)
+            pass_on(MERGED, step, way)
+    for step in range(2):
+        rows = pl.ds(step * chunk, chunk)
+        for way in range(2):
+            total[rows, pl.ds((1 - way) * half_cols, half_cols)] += arrived(DIRECT, step, way)
+    for step in range(2):
+        for way in range(2):
+            cols = pl.ds(way * half_cols, half_cols)
+            done = total[pl.ds(step * chunk, chunk), cols] + arrived(MERGED, step, way)
+            for low in range(HALF // 2):
+                for high in range(2):
+                    piece = done[(low * 2 + high) * SPAN:(low * 2 + high + 1) * SPAN]
+                    place = (high * HALF + step * (HALF // 2) + low) * SPAN
+                    out[pl.ds(place, SPAN), cols] = piece.astype(BF16)
     settled(tok_send, send_sem.at[0])
     settled(spec_send, send_sem.at[1])
     settled(back_send, send_sem.at[2])
     three = weight.at[:, pl.ds(0, 3 * half_k), :]
     pltpu.make_async_copy(three, three, weight_sem.at[SIDE]).wait()
     pltpu.make_async_copy(three, three, pair_sem.at[SIDE]).wait()
-    sent = gated.at[:, pl.ds(0, 3 * width)]
-    pltpu.make_async_copy(sent, sent, gated_sem.at[SIDE]).wait()
-    sent = part_send.at[pl.ds(0, 3)]
-    pltpu.make_async_copy(sent, sent, part_sem.at[SIDE]).wait()
+    for step in range(2):
+        sent = gated.at[pl.ds(step * chunk, chunk), pl.ds(0, 3 * width)]
+        pltpu.make_async_copy(sent, sent, gated_sem.at[step, SIDE]).wait()
+    pltpu.make_async_copy(part_send, part_send, part_sem.at[3, 0, 0]).wait()
 
 
 def layer(values, gate_in, gate_out, spectrum, out_weight):
@@ -318,15 +363,16 @@
         pltpu.VMEM((SIDE, SIDE * width, cols_each), BF16),
         pltpu.VMEM((rows, SIDE * width), BF16),
         pltpu.VMEM((rows, cols_each), F32),
-        pltpu.VMEM((SIDE, rows, cols_each), BF16),
-        pltpu.VMEM((SIDE, rows, cols_each), BF16),
+        pltpu.VMEM((2, 2, rows // 2, cols_each // 2), F32),
+        pltpu.VMEM((3, 2, 2, rows // 2, cols_each // 2), BF16),
+        pltpu.VMEM((3, 2, 2, rows // 2, cols_each // 2), BF16),
         pltpu.SemaphoreType.DMA((len(loaded) + 1 + SIDE,)),
         pltpu.SemaphoreType.DMA((3,)),
         pltpu.SemaphoreType.DMA((3,)),
         pltpu.SemaphoreType.DMA((SIDE + 1,)),
         pltpu.SemaphoreType.DMA((SIDE + 1,)),
-        pltpu.SemaphoreType.DMA((SIDE + 1,)),
-        pltpu.SemaphoreType.DMA((SIDE + 1,)),
+        pltpu.SemaphoreType.DMA((2, SIDE + 1)),
+        pltpu.SemaphoreType.DMA((4, 2, 2)),
     ]
     return pl.pallas_call(
         layer_kernel,

time: 97.1 us -> 84.1 us (0.87)
  Pallas kernels: 94.5 us -> 81.2 us
    pallas_call x1, Pallas kernels: 94.5 us -> 81.2 us  [layer(): pl.pallas_call(layer_kernel, out_shape=jax.ShapeDtypeStruct((rows, cols_e...]
where the time goes in v3:
time: 84.1 us; the launch traced here: 82.9 us
  Pallas kernels  81.2 us (97%)
  local copies, waits for them, and re-layouts  1.67 us (2%)
    pallas_call x1, Pallas kernels, layer(): pl.pallas_call(layer_kernel, out_shape=jax.ShapeDtypeStruct((rows, cols_e...  81.2 us

profile of v3, /device:TPU:1, one launch (start us, length us, event | category | flops | bytes accessed | tf_op | source)
XLA Modules:
  0.0 82.9 jit_solution(10517027496405476486)
XLA Ops:
  0.0 81.2 %layer.1 = bf16[256,512]{1,0:T(8,128)(2,1)} custom-call(bf16[256,256]{1,0:T(8,128)(2,1)} %values_h.1, bf16[256,256]{1,0:T(8,128)(2,1)} %gate_in_h.1, bf16[256,256]{1,0:T(8,128)(2,1)} %gate_out_h.1, f32[512,256]{1,0:T(8,128)} %bitcast.1, bf16[256,8192]{1,0:T(8,128)(2,1)} %weight_h.1, bf16[2048,512]{1,0:T(8,128)(2,1)} %constant.16.clone.forward_h, ...), custom_call_target="tpu_custom_call" | custom-call | tf_op jit(solution)/shard_map/layer/pallas_call | solution.py:377
  81.2 1.7 %copy.15 = bf16[256,512]{1,0:T(8,128)(2,1)} copy(bf16[256,512]{1,0:T(8,128)(2,1)} %layer.1) | data formatting | bytes 524288

commit v4 on v3

--- a/solution.py
+++ b/solution.py
@@ -19,6 +19,7 @@
 SIDE = 4
 OWN = 4
 FAR, DIRECT, MERGED = range(3)
+STEPS = 4
 MESH = pl.DeviceIdType.MESH
 BF16 = jnp.bfloat16
 F32 = jnp.float32
@@ -80,6 +81,25 @@
     col_x, col_y = lax.rem(group, SIDE), group // SIDE
     core = lax.rem(me, 2)
     sibling = me + 1 - 2 * core
+    barrier = pltpu.get_barrier_semaphore()
+
+    def far_first(i):
+        return lax.rem(me + SEQ // 2 + ((i + 1) // 2) * (1 - 2 * lax.rem(i, 2)), SEQ)
+
+    @pl.loop(0, SEQ - 1)
+    def _(i):
+        pl.semaphore_signal(barrier, inc=1, device_id={"seq": far_first(i)}, device_id_type=MESH)
+
+    def at_x(i):
+        return col_y * SIDE + lax.rem(col_x + i, SIDE)
+
+    def at_y(i):
+        return lax.rem(col_y + i, SIDE) * SIDE + col_x
+
+    for i in range(1, SIDE):
+        for peer in (at_x(i), at_y(i)):
+            pl.semaphore_signal(barrier, inc=1, device_id={"chan": peer}, device_id_type=MESH)
+
     sources = (values_h, gate_in_h, pick_h, forward_h, twist_h, mix_h, unmix_h, inverse_h,
                gate_out_h, pick_t_h, fold_h)
     targets = (values, gate_in, pick, forward, twist, mix, unmix, inverse,
@@ -107,32 +127,13 @@
 
     for i in range(SIDE):
         own_weight(i).start()
-    barrier = pltpu.get_barrier_semaphore()
-
-    @pl.loop(1, SEQ)
-    def _(i):
-        pl.semaphore_signal(
-            barrier, inc=1, device_id={"seq": lax.rem(me + i, SEQ)}, device_id_type=MESH
-        )
-
-    def at_x(i):
-        return col_y * SIDE + lax.rem(col_x + i, SIDE)
-
-    def at_y(i):
-        return lax.rem(col_y + i, SIDE) * SIDE + col_x
-
-    for i in range(1, SIDE):
-        for peer in (at_x(i), at_y(i)):
-            pl.semaphore_signal(barrier, inc=1, device_id={"chan": peer}, device_id_type=MESH)
-
-    def exchange(send, recv, slot):
+    def exchange(send, recv, slot, quarter):
         @pl.loop(0, SEQ - 1)
         def _(i):
-            away = SEQ // 2 + ((i + 1) // 2) * (1 - 2 * lax.rem(i, 2))
-            peer = lax.rem(me + away, SEQ)
+            peer = far_first(i)
             pltpu.make_async_remote_copy(
                 src_ref=send.at[peer], dst_ref=recv.at[me],
-                send_sem=send_sem.at[slot], recv_sem=recv_sem.at[slot],
+                send_sem=send_sem.at[slot], recv_sem=recv_sem.at[slot, quarter],
                 device_id={"seq": peer}, device_id_type=MESH,
             ).start()
 
@@ -154,22 +155,6 @@
         spread = jnp.concatenate(pieces, axis=0).astype(BF16)
         stage[pl.ds(low, SEQ, stride=HALF), :] = dot_t(picked, spread)
     tok_send[...] = stage[...].reshape(SEQ, HALF, LANES).astype(BF16)
-    pl.semaphore_wait(barrier, SEQ - 1 + 2 * (SIDE - 1))
-    exchange(tok_send, tok_recv, 0)
-    tok_recv[me] = tok_send[me]
-    half_rows = pl.multiple_of(core * half_k, half_k)
-
-    @pl.loop(0, SIDE)
-    def _(i):
-        for j in range(1, SIDE):
-            cols = pl.multiple_of((i * SIDE + lax.rem(col_x + j, SIDE)) * cols_each, cols_each)
-            rows = pl.multiple_of(col_x * 2 * half_k + half_rows, half_k)
-            pltpu.make_async_remote_copy(
-                src_ref=weight_h.at[pl.ds(half_rows, half_k), pl.ds(cols, cols_each)],
-                dst_ref=weight.at[i, pl.ds(rows, half_k), :],
-                send_sem=weight_sem.at[SIDE], recv_sem=weight_sem.at[col_x],
-                device_id={"chan": at_x(j)}, device_id_type=MESH,
-            ).start()
     for load in halves:
         load.wait()
     for col in range(SPAN):
@@ -182,11 +167,27 @@
         spread = jnp.concatenate(pieces, axis=0).astype(BF16)
         wide[pl.ds(col, SEQ, stride=SPAN), :] = dot_t(picked, spread)
     spec_send[...] = wide[...].reshape(SEQ, SPAN, LANES).astype(BF16)
-    exchange(spec_send, spec_recv, 1)
+    pl.semaphore_wait(barrier, SEQ - 1 + 2 * (SIDE - 1))
+    exchange(tok_send, tok_recv, 0, 0)
+    tok_recv[me] = tok_send[me]
+    exchange(spec_send, spec_recv, 1, me // 16)
     spec_recv[me] = spec_send[me]
+    half_rows = pl.multiple_of(core * half_k, half_k)
+
+    @pl.loop(0, SIDE)
+    def _(i):
+        for j in range(1, SIDE):
+            cols = pl.multiple_of((i * SIDE + lax.rem(col_x + j, SIDE)) * cols_each, cols_each)
+            rows = pl.multiple_of(col_x * 2 * half_k + half_rows, half_k)
+            pltpu.make_async_remote_copy(
+                src_ref=weight_h.at[pl.ds(half_rows, half_k), pl.ds(cols, cols_each)],
+                dst_ref=weight.at[i, pl.ds(rows, half_k), :],
+                send_sem=weight_sem.at[SIDE], recv_sem=weight_sem.at[col_x],
+                device_id={"chan": at_x(j)}, device_id_type=MESH,
+            ).start()
     for load in loads[3:]:
         load.wait()
-    settled(tok_recv, recv_sem.at[0])
+    settled(tok_recv, recv_sem.at[0, 0])
     columns = tok_recv[...].reshape(SEQ * HALF, LANES)
     step = 256
 
@@ -199,13 +200,13 @@
         pair = jnp.concatenate([re * tr - im * ti, re * ti + im * tr], axis=1).astype(BF16)
         freq[rows, :] = dot(pair, mix[...])
 
-    settled(spec_recv, recv_sem.at[1])
-
-    @pl.loop(0, BLOCK // step)
-    def _(i):
-        rows = pl.ds(pl.multiple_of(i * step, step), step)
-        im_rows = pl.ds(pl.multiple_of(BLOCK + i * step, step), step)
-        filt = spec_recv[pl.ds(i * (step // SPAN), step // SPAN)].reshape(step, LANES).astype(F32)
+    for turn in (2, 1, 3, 0):
+        quarter = lax.rem(me // 16 + turn, 4)
+        got = spec_recv.at[pl.ds(0, 16 if turn else 15)]
+        pltpu.make_async_copy(got, got, recv_sem.at[1, quarter]).wait()
+        rows = pl.ds(pl.multiple_of(quarter * step, step), step)
+        im_rows = pl.ds(pl.multiple_of(BLOCK + quarter * step, step), step)
+        filt = spec_recv[pl.ds(quarter * 16, 16)].reshape(step, LANES).astype(F32)
         prod = freq[rows, :LANES] * filt + freq[rows, LANES:] * pltpu.roll(filt, 64, 1)
         back = dot(prod.astype(BF16), unmix[...])
         re, im = back[:, :LANES], back[:, LANES:]
@@ -224,7 +225,7 @@
             peer = first + lax.rem(me + i, 16)
             pltpu.make_async_remote_copy(
                 src_ref=back_send.at[peer], dst_ref=back_recv.at[me],
-                send_sem=send_sem.at[2], recv_sem=recv_sem.at[2],
+                send_sem=send_sem.at[2], recv_sem=recv_sem.at[2, 0],
                 device_id={"seq": peer}, device_id_type=MESH,
             ).start()
 
@@ -243,7 +244,7 @@
             device_id={"seq": sibling}, device_id_type=MESH,
         ).start()
 
-    settled(back_recv, recv_sem.at[2])
+    settled(back_recv, recv_sem.at[2, 0])
     stage[...] = back_recv[...].reshape(SEQ * HALF, LANES).astype(F32)
     chan_row = lax.rem(lax.broadcasted_iota(jnp.int32, (SEQ * OWN, LANES), 0), OWN)
     chan_lane = lax.rem(lax.broadcasted_iota(jnp.int32, (SEQ * OWN, LANES), 1) // SPAN, OWN)
@@ -263,7 +264,7 @@
             [gate_out[pl.ds((high * HALF + low) * SPAN, SPAN), :] for high in range(2)], axis=0
         ).astype(F32)
         gated[pl.ds(low * 2 * SPAN, 2 * SPAN), own_cols] = (conv * gate).astype(BF16)
-        step, done = divmod(low + 1, HALF // 2)
+        step, done = divmod(low + 1, HALF // STEPS)
         if done == 0:
             for i in (2, 1, 3):
                 pltpu.make_async_remote_copy(
@@ -291,7 +292,7 @@
         return ref[...].astype(F32)
 
     half_cols = cols_each // 2
-    for step in range(2):
+    for step in range(STEPS):
         for i in (1, 3, 2):
             part = gated_part(step, lax.rem(col_x + i, SIDE))
             pltpu.make_async_copy(part, part, gated_sem.at[step, lax.rem(col_x + i, SIDE)]).wait()
@@ -311,22 +312,22 @@
             kept[step, way] = block_half(away, way)
         for half in range(2):
             total[rows, pl.ds(half * half_cols, half_cols)] = block_half(0, half)
-    for step in range(2):
+    for step in range(STEPS):
         for way in range(2):
             part_send[MERGED, step, way] = (kept[step, way] + arrived(FAR, step, way)).astype(BF16)
             pass_on(MERGED, step, way)
-    for step in range(2):
+    for step in range(STEPS):
         rows = pl.ds(step * chunk, chunk)
         for way in range(2):
             total[rows, pl.ds((1 - way) * half_cols, half_cols)] += arrived(DIRECT, step, way)
-    for step in range(2):
+    for step in range(STEPS):
         for way in range(2):
             cols = pl.ds(way * half_cols, half_cols)
             done = total[pl.ds(step * chunk, chunk), cols] + arrived(MERGED, step, way)
-            for low in range(HALF // 2):
+            for low in range(HALF // STEPS):
                 for high in range(2):
                     piece = done[(low * 2 + high) * SPAN:(low * 2 + high + 1) * SPAN]
-                    place = (high * HALF + step * (HALF // 2) + low) * SPAN
+                    place = (high * HALF + step * (HALF // STEPS) + low) * SPAN
                     out[pl.ds(place, SPAN), cols] = piece.astype(BF16)
     settled(tok_send, send_sem.at[0])
     settled(spec_send, send_sem.at[1])
@@ -334,7 +335,7 @@
     three = weight.at[:, pl.ds(0, 3 * half_k), :]
     pltpu.make_async_copy(three, three, weight_sem.at[SIDE]).wait()
     pltpu.make_async_copy(three, three, pair_sem.at[SIDE]).wait()
-    for step in range(2):
+    for step in range(STEPS):
         sent = gated.at[pl.ds(step * chunk, chunk), pl.ds(0, 3 * width)]
         pltpu.make_async_copy(sent, sent, gated_sem.at[step, SIDE]).wait()
     pltpu.make_async_copy(part_send, part_send, part_sem.at[3, 0, 0]).wait()
@@ -363,16 +364,16 @@
         pltpu.VMEM((SIDE, SIDE * width, cols_each), BF16),
         pltpu.VMEM((rows, SIDE * width), BF16),
         pltpu.VMEM((rows, cols_each), F32),
-        pltpu.VMEM((2, 2, rows // 2, cols_each // 2), F32),
-        pltpu.VMEM((3, 2, 2, rows // 2, cols_each // 2), BF16),
-        pltpu.VMEM((3, 2, 2, rows // 2, cols_each // 2), BF16),
+        pltpu.VMEM((STEPS, 2, rows // STEPS, cols_each // 2), F32),
+        pltpu.VMEM((3, STEPS, 2, rows // STEPS, cols_each // 2), BF16),
+        pltpu.VMEM((3, STEPS, 2, rows // STEPS, cols_each // 2), BF16),
         pltpu.SemaphoreType.DMA((len(loaded) + 1 + SIDE,)),
         pltpu.SemaphoreType.DMA((3,)),
-        pltpu.SemaphoreType.DMA((3,)),
+        pltpu.SemaphoreType.DMA((3, 4)),
         pltpu.SemaphoreType.DMA((SIDE + 1,)),
         pltpu.SemaphoreType.DMA((SIDE + 1,)),
-        pltpu.SemaphoreType.DMA((2, SIDE + 1)),
-        pltpu.SemaphoreType.DMA((4, 2, 2)),
+        pltpu.SemaphoreType.DMA((STEPS, SIDE + 1)),
+        pltpu.SemaphoreType.DMA((4, STEPS, 2)),
     ]
     return pl.pallas_call(
         layer_kernel,

time: 84.1 us -> 83 us (0.987)
  the two profiles are of different devices: /device:TPU:1 before, /device:TPU:64 now
where the time goes in v4:
time: 83 us; the launch traced here: 82.8 us
  Pallas kernels  81.1 us (98%)
  local copies, waits for them, and re-layouts  1.67 us (2%)
    pallas_call x1, Pallas kernels, layer(): pl.pallas_call(layer_kernel, out_shape=jax.ShapeDtypeStruct((rows, cols_e...  81.1 us
    unnamed x1, local copies, waits for them, and re-layouts  1.67 us

profile of v4, /device:TPU:64, one launch (start us, length us, event | category | flops | bytes accessed | tf_op | source)
XLA Modules:
  0.0 82.8 jit_solution(5253791982724426763)
XLA Ops:
  0.0 81.1 %layer.1 = bf16[256,512]{1,0:T(8,128)(2,1)} custom-call(bf16[256,256]{1,0:T(8,128)(2,1)} %values_h.1, bf16[256,256]{1,0:T(8,128)(2,1)} %gate_in_h.1, bf16[256,256]{1,0:T(8,128)(2,1)} %gate_out_h.1, f32[512,256]{1,0:T(8,128)} %bitcast.1, bf16[256,8192]{1,0:T(8,128)(2,1)} %weight_h.1, bf16[2048,512]{1,0:T(8,128)(2,1)} %constant.16.clone.forward_h, ...), custom_call_target="tpu_custom_call" | custom-call | tf_op jit(solution)/shard_map/layer/pallas_call | solution.py:378
  81.1 1.7 %copy.15 = bf16[256,512]{1,0:T(8,128)(2,1)} copy(bf16[256,512]{1,0:T(8,128)(2,1)} %layer.1) | data formatting | bytes 524288

commit v5 on v4

--- a/solution.py
+++ b/solution.py
@@ -382,11 +382,16 @@
         out_specs=pl.BlockSpec(memory_space=pltpu.VMEM),
         scratch_shapes=scratch,
         compiler_params=pltpu.CompilerParams(
-            collective_id=0, has_side_effects=True, vmem_limit_bytes=60 << 20
+            collective_id=0, has_side_effects=True, vmem_limit_bytes=32 << 20
         ),
         name="layer",
-    )(values, gate_in, gate_out, flat, out_weight, *[jnp.asarray(t) for t in
-      (forward, inverse, twist, mix, unmix, pick, pick_t, fold)])
+    )(*[
+        pltpu.with_memory_space_constraint(t, pltpu.HBM)
+        for t in (values, gate_in, gate_out, flat, out_weight)
+    ], *[
+        pltpu.with_memory_space_constraint(jnp.asarray(t), pltpu.HBM)
+        for t in (forward, inverse, twist, mix, unmix, pick, pick_t, fold)
+    ])
 
 
 def solution(mesh):

time: 83 us -> 81.3 us (0.980)
  local copies, waits for them, and re-layouts: 1.67 us -> 0.71 us
    unnamed x1, local copies, waits for them, and re-layouts: 1.67 us -> 0.71 us
where the time goes in v5:
time: 81.3 us; the launch traced here: 81.1 us
  Pallas kernels  80.4 us (99%)
    pallas_call x1, Pallas kernels, layer(): pl.pallas_call(layer_kernel, out_shape=jax.ShapeDtypeStruct((rows, cols_e...  80.4 us

profile of v5, /device:TPU:64, one launch (start us, length us, event | category | flops | bytes accessed | tf_op | source)
XLA Modules:
  0.0 81.1 jit_solution(763274995293425462)
XLA Ops:
  0.0 80.4 %layer.1 = bf16[256,512]{1,0:T(8,128)(2,1)S(1)} custom-call(bf16[256,256]{1,0:T(8,128)(2,1)} %values_h.1, bf16[256,256]{1,0:T(8,128)(2,1)} %gate_in_h.1, bf16[256,256]{1,0:T(8,128)(2,1)} %gate_out_h.1, f32[512,256]{1,0:T(8,128)} %bitcast.1, bf16[256,8192]{1,0:T(8,128)(2,1)} %weight_h.1, bf16[2048,512]{1,0:T(8,128)(2,1)} %constant.16.clone.forward_h, ...), custom_call_target="tpu_custom_call" | custom-call | tf_op jit(solution)/shard_map/layer/pallas_call | solution.py:378
  80.4 0.7 copy.15

commit v6 on v5

--- a/solution.py
+++ b/solution.py
@@ -235,15 +235,6 @@
         rows = pl.multiple_of(source * 2 * half_k + which * half_k, half_k)
         return weight.at[:, pl.ds(rows, half_k), :]
 
-    for i in (1, 3, 2):
-        source = lax.rem(col_x + i, SIDE)
-        mine = weight_half(source, core)
-        pltpu.make_async_copy(mine, mine, weight_sem.at[source]).wait()
-        pltpu.make_async_remote_copy(
-            src_ref=mine, dst_ref=mine, send_sem=pair_sem.at[SIDE], recv_sem=pair_sem.at[source],
-            device_id={"seq": sibling}, device_id_type=MESH,
-        ).start()
-
     settled(back_recv, recv_sem.at[2, 0])
     stage[...] = back_recv[...].reshape(SEQ * HALF, LANES).astype(F32)
     chan_row = lax.rem(lax.broadcasted_iota(jnp.int32, (SEQ * OWN, LANES), 0), OWN)
@@ -272,6 +263,17 @@
                     send_sem=gated_sem.at[step - 1, SIDE], recv_sem=gated_sem.at[step - 1, col_x],
                     device_id={"chan": at_x(i)}, device_id_type=MESH,
                 ).start()
+    for i in (1, 3, 2):
+        source = lax.rem(col_x + i, SIDE)
+        mine = weight_half(source, core)
+        pltpu.make_async_copy(mine, mine, weight_sem.at[source]).wait()
+        rows = pl.ds(pl.multiple_of(source * 2 * half_k + half_rows, half_k), half_k)
+        for block in range(SIDE):
+            pltpu.make_async_remote_copy(
+                src_ref=weight.at[block, rows, :], dst_ref=weight.at[block, rows, :],
+                send_sem=pair_sem.at[SIDE], recv_sem=pair_sem.at[source],
+                device_id={"seq": sibling}, device_id_type=MESH,
+            ).start()
     for i in range(SIDE):
         own_weight(i).wait()
     for i in (1, 3, 2):

time: 81.3 us -> 80.9 us (level)
  the two profiles are of different devices: /device:TPU:64 before, /device:TPU:1 now
where the time goes in v6:
time: 80.9 us; the launch traced here: 80.4 us
  Pallas kernels  79.7 us (99%)
    pallas_call x1, Pallas kernels, layer(): pl.pallas_call(layer_kernel, out_shape=jax.ShapeDtypeStruct((rows, cols_e...  79.7 us

profile of v6, /device:TPU:1, one launch (start us, length us, event | category | flops | bytes accessed | tf_op | source)
XLA Modules:
  0.0 80.4 jit_solution(7594122859745852940)
XLA Ops:
  0.0 79.7 %layer.1 = bf16[256,512]{1,0:T(8,128)(2,1)S(1)} custom-call(bf16[256,256]{1,0:T(8,128)(2,1)} %values_h.1, bf16[256,256]{1,0:T(8,128)(2,1)} %gate_in_h.1, bf16[256,256]{1,0:T(8,128)(2,1)} %gate_out_h.1, f32[512,256]{1,0:T(8,128)} %bitcast.1, bf16[256,8192]{1,0:T(8,128)(2,1)} %weight_h.1, bf16[2048,512]{1,0:T(8,128)(2,1)} %constant.16.clone.forward_h, ...), custom_call_target="tpu_custom_call" | custom-call | tf_op jit(solution)/shard_map/layer/pallas_call | solution.py:380
  79.7 0.7 copy.15
